TPU v7x, 32 devices: a whole 2x2x4 slice. The times are simulated.
32 devices in a mesh: row: 8 (over y, x, core), col: 4 (over z).
Axes of the slice: x: 2, y: 2, z: 4, core: 2. Of those that a mesh axis runs over, the one named last changes fastest.
Arguments:
- gradient: bfloat16 [24576, 24576], P('row', 'col'), may hold values from -6 to 6
- sensitivity: bfloat16 [24576, 16384], P('row', 'col'), may hold values from -0.0390625 to 0.0390625
Outputs:
- influence: float32 [512, 16384], P('row', 'col')
All inputs are finite; a program needn't handle non-finite values.
Results may differ from a plain program's by a relative error of at most 0.0029.
Values may be sent and summed in bfloat16 or wider, within the bound.
A program may use at most 128 MiB of HBM per device.

v0:
```python
import jax
import jax.numpy as jnp
from jax import lax
from jax.sharding import PartitionSpec as P

PANEL = 512


def from_root(value, axis, root):
    mine = lax.axis_index(axis) == root
    return lax.psum(jnp.where(mine, value, jnp.zeros_like(value)), axis)


def shards(gradient, sensitivity):
    ratio = lax.axis_size("row") // lax.axis_size("col")
    own_panel = sensitivity[:, :PANEL]
    panel_here = from_root(own_panel, "col", 0)
    col_index = lax.axis_index("col")
    pieces = []
    for member in range(ratio):
        pieces.append(from_root(panel_here, "row", col_index * ratio + member))
    panel_block = jnp.concatenate(pieces, axis=0)
    partial_value = jnp.dot(gradient, panel_block, preferred_element_type=jnp.float32)
    image = lax.psum(partial_value, "col").astype(jnp.bfloat16)
    return lax.psum_scatter(
        lax.dot_general(
            image, sensitivity, (((0,), (0,)), ((), ())), preferred_element_type=jnp.float32
        ),
        "row",
        scatter_dimension=0,
        tiled=True,
    )


def solution(mesh):
    return jax.shard_map(
        shards,
        mesh=mesh,
        in_specs=(P("row", "col"), P("row", "col")),
        out_specs=P("row", "col"),
        check_vma=False,
    )
```

profile of v0, /device:TPU:0, one launch (start us, length us, event | category | flops | bytes accessed | tf_op | source)
XLA Modules:
  0.0 583.4 jit_solution(8317482870267149150)
XLA Ops:
  6.5 0.0 all-reduce.5.cloned.1.call-start
  6.5 3.8 slice_select_fusion
  10.3 0.0 all-reduce.5.cloned.1.call-update
  10.3 0.0 all-reduce.7.cloned.1.call-start
  10.4 123.9 %all-reduce.5.cloned.1.call-done = bf16[3072,512]{1,0:T(8,128)(2,1)} async-done(((bf16[3072,512]{1,0:T(8,128)(2,1)}), bf16[3072,512]{1,0:T(8,128)(2,1)}) %all-reduce.5.cloned.1.call-update) | async-done | bytes 3145744 | tf_op jit(solution)/shard_map/psum | solution.py:11
  134.3 5.0 broadcast_select_fusion.1
  139.2 0.0 all-reduce.7.cloned.1.call-update
  139.2 0.0 reduce-scatter.2.cloned.1.call-start
  139.3 103.5 %all-reduce.7.cloned.1.call-done = (bf16[3072,512]{1,0:T(8,128)(2,1)}, bf16[3072,512]{1,0:T(8,128)(2,1)}) async-done(((bf16[3072,512]{1,0:T(8,128)(2,1)}, bf16[3072,512]{1,0:T(8,128)(2,1)}), (bf16[3072,512]{1,0:T(8,128)(2,1)}, bf16[3072,512]{1,0:T(8,128)(2,1)})) %all-reduce.7.cloned.1.call-update) | async-done | bytes 6291472 | tf_op jit(solution)/shard_map/psum | solution.py:11
  242.8 27.1 %fusion.4 = f32[3072,512]{0,1:T(8,128)} fusion(bf16[3072,6144]{1,0:T(8,128)(2,1)} %param.2, bf16[3072,512]{1,0:T(8,128)(2,1)} %get-tuple-element.5, bf16[3072,512]{1,0:T(8,128)(2,1)} %get-tuple-element.6), kind=kOutput, calls=%fused_computation.4 | convolution fusion | flops 19339935744 | bytes 50331648 | tf_op jit(solution)/shard_map/dot_general | solution.py:23
  269.9 217.7 %all-reduce.8 = bf16[3072,512]{0,1:T(8,128)(2,1)S(1)} all-reduce(f32[3072,512]{0,1:T(8,128)} %fusion.4), channel_id=1, replica_groups=mesh['row'=8,'col'=4] {'col'}, use_global_device_ids=true, to_apply=%region_3.4 | all-reduce | flops 1572864 | bytes 9437184 | tf_op jit(solution)/shard_map/psum | solution.py:24
  487.5 19.9 %fusion.10 = f32[512,4096]{1,0:T(8,128)} fusion(bf16[3072,512]{0,1:T(8,128)(2,1)S(1)} %all-reduce.8, bf16[3072,4096]{1,0:T(8,128)(2,1)} %param.3), kind=kOutput, calls=%fused_computation.11 | convolution fusion | flops 12884901888 | bytes 36700160 | tf_op jit(solution)/shard_map/dot_general | solution.py:26
  507.4 0.0 reduce-scatter.2.cloned.1.call-update
  507.4 69.4 %reduce-scatter.2.cloned.1.call-done = f32[64,4096]{1,0:T(8,128)} async-done(((f32[512,4096]{1,0:T(8,128)}), f32[64,4096]{1,0:T(8,128)}) %reduce-scatter.2.cloned.1.call-update) | async-done | bytes 1048592 | tf_op jit(solution)/shard_map/reduce_scatter | solution.py:25
Async XLA Ops:
  6.5 127.7 %all-reduce.5.cloned.1.call-start = ((), (), s32[]{:S(2)}) async-start(), calls=%async_computation.1 | async-start | bytes 6291456 | tf_op jit(solution)/shard_map/psum | solution.py:11
  10.3 232.5 %all-reduce.7.cloned.1.call-start = ((), (), s32[]{:S(2)}) async-start(), calls=%async_computation.3 | async-start | bytes 12582912 | tf_op jit(solution)/shard_map/psum | solution.py:11
  139.2 437.6 %reduce-scatter.2.cloned.1.call-start = ((), (), s32[]{:S(2)}) async-start(), calls=%async_computation.2 | async-start | bytes 9437184 | tf_op jit(solution)/shard_map/reduce_scatter | solution.py:25
Sparse Core Ops, SparseCore 0:
  10.4 123.7 all-reduce.4
  139.4 103.3 all-reduce.6
  507.6 69.2 reduce-scatter.1
where the time goes:
time: 584 us; the launch traced here: 583 us
  waiting for transfers between devices  297 us (51%)
  blocking collectives  218 us (37%)
  matrix products  47 us (8%)
  between operations  13.1 us (2%)
  other arithmetic  8.71 us (1%)
    psum x2, waiting for transfers between devices, from_root(): return lax.psum(jnp.where(mine, value, jnp.zeros_like(value)), axis)  227 us
    psum x1, blocking collectives, shards(): image = lax.psum(partial_value, 'col').astype(jnp.bfloat16)  218 us
    reduce_scatter x1, waiting for transfers between devices, shards(): lax.psum_scatter(lax.dot_general(image, sensitivity, (((0,), (0,)), ((),...  69.4 us
    dot_general x1, matrix products, shards(): jnp.dot(gradient, panel_block, preferred_element_type=jnp.float32)  27.1 us
    dot_general x1, matrix products, shards(): lax.dot_general(image, sensitivity, (((0,), (0,)), ((), ())), preferred_e...  19.9 us
  transfers between devices with their start and end apart: 3, of which 3 were waited for; matrix products, arithmetic and copies ran while one was open for 0% of the time, Pallas kernels for 0%

commit v1 on v0

--- a/solution.py
+++ b/solution.py
@@ -4,6 +4,12 @@
 from jax.sharding import PartitionSpec as P
 
 PANEL = 512
+
+
+def summed_here(x, name):
+    pieces = lax.all_gather(x, name, axis=0, tiled=False)
+    acc = pieces.sum(axis=0)
+    return acc
 
 
 def from_root(value, axis, root):
@@ -21,7 +27,7 @@
         pieces.append(from_root(panel_here, "row", col_index * ratio + member))
     panel_block = jnp.concatenate(pieces, axis=0)
     partial_value = jnp.dot(gradient, panel_block, preferred_element_type=jnp.float32)
-    image = lax.psum(partial_value, "col").astype(jnp.bfloat16)
+    image = summed_here(partial_value, "col").astype(jnp.bfloat16)
     return lax.psum_scatter(
         lax.dot_general(
             image, sensitivity, (((0,), (0,)), ((), ())), preferred_element_type=jnp.float32

time: 584 us -> 840 us (1.44)
  waiting for transfers between devices: 297 us -> 722 us
  blocking collectives: 218 us -> 0 us
  local copies, waits for them, and re-layouts: 0 us -> 29.1 us
  other arithmetic: 8.71 us -> 27.6 us
    all_gather x0 -> x1, waiting for transfers between devices: none -> 425 us  [summed_here(): pieces = lax.all_gather(x, name, axis=0, tiled=False)]
    psum x1 -> x0, blocking collectives: 218 us -> none  [shards(): image = lax.psum(partial_value, 'col').astype(jnp.bfloat16)]
    all_gather x0 -> x1, local copies, waits for them, and re-layouts: none -> 29.1 us  [summed_here(): pieces = lax.all_gather(x, name, axis=0, tiled=False)]
    reduce_sum x0 -> x1, other arithmetic: none -> 18.9 us  [summed_here(): acc = pieces.sum(axis=0)]
  transfers between devices with their start and end apart: 3 -> 4, of which waited for: 3 -> 4; matrix products, arithmetic and copies ran while one was open for 0% -> 0% of each run, Pallas kernels for 0% -> 0%
where the time goes in v1:
time: 840 us; the launch traced here: 839 us
  waiting for transfers between devices  722 us (86%)
  matrix products  46.9 us (6%)
  local copies, waits for them, and re-layouts  29.1 us (3%)
  other arithmetic  27.6 us (3%)
  between operations  13.1 us (2%)
    all_gather x1, waiting for transfers between devices, summed_here(): pieces = lax.all_gather(x, name, axis=0, tiled=False)  425 us
    psum x2, waiting for transfers between devices, from_root(): return lax.psum(jnp.where(mine, value, jnp.zeros_like(value)), axis)  227 us
    reduce_scatter x1, waiting for transfers between devices, shards(): lax.psum_scatter(lax.dot_general(image, sensitivity, (((0,), (0,)), ((),...  69.6 us
    all_gather x1, local copies, waits for them, and re-layouts, summed_here(): pieces = lax.all_gather(x, name, axis=0, tiled=False)  29.1 us
    dot_general x1, matrix products, shards(): jnp.dot(gradient, panel_block, preferred_element_type=jnp.float32)  27 us
    dot_general x1, matrix products, shards(): lax.dot_general(image, sensitivity, (((0,), (0,)), ((), ())), preferred_e...  19.9 us
    reduce_sum x1, other arithmetic, summed_here(): acc = pieces.sum(axis=0)  18.9 us
  transfers between devices with their start and end apart: 4, of which 4 were waited for; matrix products, arithmetic and copies ran while one was open for 0% of the time, Pallas kernels for 0%

profile of v1, /device:TPU:0, one launch (start us, length us, event | category | flops | bytes accessed | tf_op | source)
XLA Modules:
  0.0 839.2 jit_solution(9607087568853091443)
XLA Ops:
  6.5 0.0 all-reduce.4.cloned.1.call-start
  6.5 3.8 slice_select_fusion
  10.3 0.0 all-reduce.4.cloned.1.call-update
  10.3 0.0 all-reduce.6.cloned.1.call-start
  10.4 123.9 %all-reduce.4.cloned.1.call-done = bf16[3072,512]{1,0:T(8,128)(2,1)} async-done(((bf16[3072,512]{1,0:T(8,128)(2,1)}), bf16[3072,512]{1,0:T(8,128)(2,1)}) %all-reduce.4.cloned.1.call-update) | async-done | bytes 3145744 | tf_op jit(solution)/shard_map/psum | solution.py:17
  134.3 5.0 broadcast_select_fusion.1
  139.2 0.0 all-reduce.6.cloned.1.call-update
  139.2 0.0 all-gather.3.cloned.1.call-start
  139.3 103.5 %all-reduce.6.cloned.1.call-done = (bf16[3072,512]{1,0:T(8,128)(2,1)}, bf16[3072,512]{1,0:T(8,128)(2,1)}) async-done(((bf16[3072,512]{1,0:T(8,128)(2,1)}, bf16[3072,512]{1,0:T(8,128)(2,1)}), (bf16[3072,512]{1,0:T(8,128)(2,1)}, bf16[3072,512]{1,0:T(8,128)(2,1)})) %all-reduce.6.cloned.1.call-update) | async-done | bytes 6291472 | tf_op jit(solution)/shard_map/psum | solution.py:17
  242.8 27.0 %fusion.4 = f32[3072,512]{0,1:T(8,128)} fusion(bf16[3072,6144]{1,0:T(8,128)(2,1)} %param.2, bf16[3072,512]{1,0:T(8,128)(2,1)} %get-tuple-element.5, bf16[3072,512]{1,0:T(8,128)(2,1)} %get-tuple-element.6), kind=kOutput, calls=%fused_computation.4 | convolution fusion | flops 19339935744 | bytes 50331648 | tf_op jit(solution)/shard_map/dot_general | solution.py:29
  269.8 0.0 all-gather.3.cloned.1.call-update
  269.8 0.2 reduce-scatter.2.cloned.1.call-start
  270.1 425.1 %all-gather.3.cloned.1.call-done = f32[12288,512]{0,1:T(8,128)} async-done(((f32[3072,512]{0,1:T(8,128)}), f32[12288,512]{0,1:T(8,128)}) %all-gather.3.cloned.1.call-update) | async-done | bytes 25165840 | tf_op jit(solution)/shard_map/all_gather | solution.py:10
  695.2 29.1 %reshape = f32[4,3072,512]{1,0,2:T(4,128)} reshape(f32[12288,512]{0,1:T(8,128)} %all-gather.3.cloned.1.call-done) | data formatting | bytes 50331648 | tf_op jit(solution)/shard_map/all_gather | solution.py:10
  724.3 18.9 %reduce_sum.9 = bf16[3072,512]{0,1:T(8,128)(2,1)S(1)} reduce(f32[4,3072,512]{1,0,2:T(4,128)} %reshape, f32[]{:T(128)} %constant.18.clone.1), dimensions={0}, to_apply=%region_3.4 | reduce | flops 4718592 | bytes 28311556 | tf_op jit(solution)/shard_map/reduce_sum | solution.py:11
  743.2 19.9 %fusion.10 = f32[512,4096]{1,0:T(8,128)} fusion(bf16[3072,512]{0,1:T(8,128)(2,1)S(1)} %reduce_sum.9, bf16[3072,4096]{1,0:T(8,128)(2,1)} %param.3), kind=kOutput, calls=%fused_computation.11 | convolution fusion | flops 12884901888 | bytes 36700160 | tf_op jit(solution)/shard_map/dot_general | solution.py:32
  763.0 0.0 reduce-scatter.2.cloned.1.call-update
  763.1 69.6 %reduce-scatter.2.cloned.1.call-done = f32[64,4096]{1,0:T(8,128)} async-done(((f32[512,4096]{1,0:T(8,128)}), f32[64,4096]{1,0:T(8,128)}) %reduce-scatter.2.cloned.1.call-update) | async-done | bytes 1048592 | tf_op jit(solution)/shard_map/reduce_scatter | solution.py:31
Async XLA Ops:
  6.5 127.7 %all-reduce.4.cloned.1.call-start = ((), (), s32[]{:S(2)}) async-start(), calls=%async_computation.1 | async-start | bytes 6291456 | tf_op jit(solution)/shard_map/psum | solution.py:17
  10.3 232.5 %all-reduce.6.cloned.1.call-start = ((), (), s32[]{:S(2)}) async-start(), calls=%async_computation.4 | async-start | bytes 12582912 | tf_op jit(solution)/shard_map/psum | solution.py:17
  139.2 556.0 %all-gather.3.cloned.1.call-start = ((), (), s32[]{:S(2)}) async-start(), calls=%async_computation.3 | async-start | bytes 31457280 | tf_op jit(solution)/shard_map/all_gather | solution.py:10
  269.8 562.9 %reduce-scatter.2.cloned.1.call-start = ((), (), s32[]{:S(2)}) async-start(), calls=%async_computation.2 | async-start | bytes 9437184 | tf_op jit(solution)/shard_map/reduce_scatter | solution.py:31
Sparse Core Ops, SparseCore 0:
  10.4 123.7 all-reduce.3
  139.4 103.3 all-reduce.5
  269.9 425.2 all-gather.2
  763.2 69.4 reduce-scatter.1
